TPU v7x, 32 devices: a whole 2x2x4 slice. The times are simulated.
32 devices in a mesh: tensor: 4 (over z), shard: 2 (over y), replica: 4 (over x, core).
Axes of the slice: x: 2, y: 2, z: 4, core: 2. Of those that a mesh axis runs over, the one named last changes fastest.
Arguments:
- block_in: float32 [8, 640, 1024], P(('shard', 'replica'), 'tensor'), may hold values from -12 to 12
- segment_ids: int32 [8, 640], P(('shard', 'replica')), may hold values from 0 to 3, never falling along the last dimension, each value on 1 to 256 neighbouring positions
- grad_out: float32 [8, 640, 1024], P(('shard', 'replica'), 'tensor'), may hold values from -6 to 6
- qkv_weight: bfloat16 [1024, 3, 1024], P('shard', None, 'tensor'), may hold values from -2 to 2
- qv_bias: bfloat16 [2, 1024], P(None, ('tensor', 'shard')), may hold values from -3 to 3
- out_weight: bfloat16 [1024, 1024], P('tensor', 'shard'), may hold values from -0.75 to 0.75
- up_weight: bfloat16 [1024, 4096], P('shard', 'tensor'), may hold values from -0.1875 to 0.1875
- up_bias: bfloat16 [4096], P(('tensor', 'shard')), may hold values from -3 to 3
- down_weight: bfloat16 [4096, 1024], P('tensor', 'shard'), may hold values from -0.09375 to 0.09375
- norm_gains: bfloat16 [2, 1024], P(None, 'shard'), may hold values from 0.25 to 1.75
- shift_biases: bfloat16 [4, 1024], P(None, 'shard'), may hold values from -3 to 3
Outputs:
- block_out: float32 [8, 640, 1024], P(('shard', 'replica'), 'tensor')
- grad_in: float32 [8, 640, 1024], P(('shard', 'replica'), 'tensor')
- grad_qkv_weight: float32 [1024, 3, 1024], P('shard', None, 'tensor')
- grad_qv_bias: float32 [2, 1024], P(None, ('tensor', 'shard'))
- grad_out_weight: float32 [1024, 1024], P('tensor', 'shard')
- grad_up_weight: float32 [1024, 4096], P('shard', 'tensor')
- grad_up_bias: float32 [4096], P(('tensor', 'shard'))
- grad_down_weight: float32 [4096, 1024], P('tensor', 'shard')
- grad_norm_gains: float32 [2, 1024], P(None, 'shard')
- grad_shift_biases: float32 [4, 1024], P(None, 'shard')
Inputs may be any that keep to these rules, and one draw needn't show every extreme that they name: segment_ids never fall along a sequence; a document has 1 to 256 tokens, and one has exactly 256.
All inputs are finite; a program needn't handle non-finite values.
Results may differ from a plain program's by a relative error of at most 0.009.
The roundings to bfloat16 on the way count: a program that leaves them out, or rounds other values in their place, can miss the bound.
Values may be sent and summed in bfloat16 or wider, within the bound.
A program may use at most 128 MiB of HBM per device.

v0:
```python
import math
import jax
import jax.numpy as jnp
from jax import lax
from jax.sharding import PartitionSpec as P

HEAD_DIM = 64
norm_eps = 1e-12
masked_score = -1e30


def norm_forward(summed, gain, shift):
    center = summed - jnp.mean(summed, axis=-1, keepdims=True)
    inverse = lax.rsqrt(jnp.mean(center * center, axis=-1, keepdims=True) + norm_eps)
    normed = center * inverse
    return (normed * gain + shift, normed, inverse)


def norm_backward(grad, normed, inverse, gain):
    scaled = grad * gain
    return inverse * (
        scaled
        - jnp.mean(scaled, axis=-1, keepdims=True)
        - normed * jnp.mean(scaled * normed, axis=-1, keepdims=True)
    )


def gelu_parts(pre_act):
    cumul = 0.5 * (1.0 + jax.scipy.special.erf(pre_act * 0.7071067811865476))
    density = jnp.exp(-0.5 * pre_act * pre_act) * 0.3989422804014327
    return (pre_act * cumul, cumul + pre_act * density)


def scatter_sum(part, axes, dim):
    return lax.psum_scatter(part.astype(jnp.bfloat16), axes, scatter_dimension=dim, tiled=True)


def shards(
    block_in,
    segment_ids,
    grad_out,
    qkv_weight,
    qv_bias,
    out_weight,
    up_weight,
    up_bias,
    down_weight,
    norm_gains,
    shift_biases,
):
    small = (qv_bias, up_bias[None], norm_gains, shift_biases)
    packed = lax.all_gather(jnp.concatenate([vec.reshape(-1) for vec in small]), "shard", axis=0)
    unpacked = []
    start = 0
    for vec in small:
        rows, piece = vec.shape
        part = packed[:, start : start + rows * piece].reshape(-1, rows, piece)
        unpacked.append(jnp.swapaxes(part, 0, 1).reshape(rows, -1))
        start += rows * piece
    qv_packed, upbias_packed, gain_packed, shift_packed = unpacked
    upbias_packed = upbias_packed[0]
    (
        query_key_value_full,
        qv_all,
        output_weight_full,
        up_weight_full,
        upbias_all,
        down_weight_full,
        gain_all,
        shift_all,
    ) = (
        lax.all_gather(qkv_weight, "shard", axis=0, tiled=True),
        qv_packed,
        lax.all_gather(out_weight, "shard", axis=1, tiled=True),
        lax.all_gather(up_weight, "shard", axis=0, tiled=True),
        upbias_packed,
        lax.all_gather(down_weight, "shard", axis=1, tiled=True),
        gain_packed,
        shift_packed,
    )
    seqs = block_in.shape[0]
    width = block_in.shape[2]
    length = segment_ids.shape[1]
    cols = query_key_value_full.shape[2]
    heads_here = cols // HEAD_DIM
    scale = 1.0 / math.sqrt(HEAD_DIM)
    gain_full = gain_all.astype(jnp.float32)
    shift_full = shift_all.astype(jnp.float32)
    qv_full = qv_all.astype(jnp.float32)
    inputs_bf = block_in.astype(jnp.bfloat16)
    input_rows_full = lax.all_gather(inputs_bf, "tensor", axis=1, tiled=True)
    query_key_value = jnp.einsum(
        "agp,pmy->agmy", input_rows_full, query_key_value_full, preferred_element_type=jnp.float32
    )
    query = (
        (query_key_value[:, :, 0] + qv_full[0])
        .astype(jnp.bfloat16)
        .reshape(seqs, length, heads_here, HEAD_DIM)
    )
    keys = query_key_value[:, :, 1].astype(jnp.bfloat16).reshape(seqs, length, heads_here, HEAD_DIM)
    values = (
        (query_key_value[:, :, 2] + qv_full[1])
        .astype(jnp.bfloat16)
        .reshape(seqs, length, heads_here, HEAD_DIM)
    )
    same = (segment_ids[:, :, None] == segment_ids[:, None, :])[:, None]
    scores = jnp.einsum("sqhe,skhe->shqk", query, keys, preferred_element_type=jnp.float32) * scale
    scores = jnp.where(same, scores, masked_score)
    highest = jnp.max(scores, axis=-1, keepdims=True)
    expo = jnp.exp(scores - highest)
    total = jnp.sum(expo, axis=-1, keepdims=True)
    probs = (expo / total).astype(jnp.bfloat16)
    log_total = highest + jnp.log(total)
    attention_context = jnp.einsum(
        "shqk,skhe->sqhe", probs, values, preferred_element_type=jnp.float32
    )
    attention_context = attention_context.astype(jnp.bfloat16).reshape(seqs, length, cols)
    attention_slice = jnp.einsum(
        "nip,pr->nir", attention_context, output_weight_full, preferred_element_type=jnp.float32
    )
    attended = scatter_sum(attention_slice, "tensor", 1).astype(jnp.float32)
    first_sum = block_in + (attended + shift_full[0])
    hidden, normed_one, inverse_one = norm_forward(first_sum, gain_full[0], shift_full[1])
    hidden_bf = hidden.astype(jnp.bfloat16)
    hidden_state_full = lax.all_gather(hidden_bf, "tensor", axis=1, tiled=True)
    pre_act = jnp.einsum(
        "peo,ot->pet", hidden_state_full, up_weight_full, preferred_element_type=jnp.float32
    ) + upbias_all.astype(jnp.float32)
    activ, slope = gelu_parts(pre_act)
    activation_bfloat = activ.astype(jnp.bfloat16)
    down_weight_slice = jnp.einsum(
        "uzt,tv->uzv", activation_bfloat, down_weight_full, preferred_element_type=jnp.float32
    )
    second_sum = hidden + (
        scatter_sum(down_weight_slice, "tensor", 1).astype(jnp.float32) + shift_full[2]
    )
    block_out, normed_two, inverse_two = norm_forward(second_sum, gain_full[1], shift_full[3])
    d_second = norm_backward(grad_out, normed_two, inverse_two, gain_full[1])
    second_gradient_full = lax.all_gather(
        d_second.astype(jnp.bfloat16), "tensor", axis=1, tiled=True
    )
    down_weight_gradient = jnp.einsum(
        "bct,bcm->tm", activation_bfloat, second_gradient_full, preferred_element_type=jnp.float32
    )
    d_pre = (
        jnp.einsum(
            "ajn,tn->ajt",
            second_gradient_full,
            down_weight_full,
            preferred_element_type=jnp.float32,
        )
        * slope
    )
    g_upbias = jnp.sum(d_pre, axis=(0, 1))
    preact_gradient_bfloat = d_pre.astype(jnp.bfloat16)
    up_weight_gradient = jnp.einsum(
        "ahk,ahp->kp", hidden_state_full, preact_gradient_bfloat, preferred_element_type=jnp.float32
    )
    hidden_state_slice = jnp.einsum(
        "ixj,gj->ixg", preact_gradient_bfloat, up_weight_full, preferred_element_type=jnp.float32
    )
    d_hidden = scatter_sum(hidden_state_slice, "tensor", 1).astype(jnp.float32) + d_second
    d_first = norm_backward(d_hidden, normed_one, inverse_one, gain_full[0])
    gain_part = jnp.stack(
        [jnp.sum(d_hidden * normed_one, axis=(0, 1)), jnp.sum(grad_out * normed_two, axis=(0, 1))]
    )
    shift_part = jnp.stack(
        [
            jnp.sum(d_first, axis=(0, 1)),
            jnp.sum(d_hidden, axis=(0, 1)),
            jnp.sum(d_second, axis=(0, 1)),
            jnp.sum(grad_out, axis=(0, 1)),
        ]
    )
    first_gradient_full = lax.all_gather(d_first.astype(jnp.bfloat16), "tensor", axis=1, tiled=True)
    output_weight_gradient = jnp.einsum(
        "unb,una->ba", attention_context, first_gradient_full, preferred_element_type=jnp.float32
    )
    context_gradient = jnp.einsum(
        "tbu,wu->tbw", first_gradient_full, output_weight_full, preferred_element_type=jnp.float32
    )
    context_gradient = context_gradient.astype(jnp.bfloat16).reshape(
        seqs, length, heads_here, HEAD_DIM
    )
    probs_back = jnp.exp(scores - log_total)
    d_probs = jnp.einsum(
        "sqhe,skhe->shqk", context_gradient, values, preferred_element_type=jnp.float32
    )
    row_dot = jnp.sum(probs_back * d_probs, axis=-1, keepdims=True)
    d_scores = (probs_back * (d_probs - row_dot)).astype(jnp.bfloat16)
    d_query = (
        jnp.einsum("shqk,skhe->sqhe", d_scores, keys, preferred_element_type=jnp.float32) * scale
    )
    d_keys = (
        jnp.einsum("shqk,sqhe->skhe", d_scores, query, preferred_element_type=jnp.float32) * scale
    )
    d_values = jnp.einsum(
        "shqk,sqhe->skhe",
        probs_back.astype(jnp.bfloat16),
        context_gradient,
        preferred_element_type=jnp.float32,
    )
    d_query = d_query.reshape(seqs, length, cols)
    d_keys = d_keys.reshape(seqs, length, cols)
    d_values = d_values.reshape(seqs, length, cols)
    g_qv = jnp.stack([jnp.sum(d_query, axis=(0, 1)), jnp.sum(d_values, axis=(0, 1))])
    projected_gradient_bfloat = jnp.stack([d_query, d_keys, d_values], axis=2).astype(jnp.bfloat16)
    projection_weight_gradient = jnp.einsum(
        "pjx,pjvy->xvy",
        input_rows_full,
        projected_gradient_bfloat,
        preferred_element_type=jnp.float32,
    )
    input_slice = jnp.einsum(
        "pxvk,yvk->pxy",
        projected_gradient_bfloat,
        query_key_value_full,
        preferred_element_type=jnp.float32,
    )
    grad_in = scatter_sum(input_slice, "tensor", 1).astype(jnp.float32) + d_first
    matrices = (
        projection_weight_gradient,
        output_weight_gradient,
        up_weight_gradient,
        down_weight_gradient,
    )
    spread = (
        scatter_sum(matrices[0], ("shard", "replica"), 0),
        scatter_sum(matrices[1], ("shard", "replica"), 1),
        scatter_sum(matrices[2], ("shard", "replica"), 0),
        scatter_sum(matrices[3], ("shard", "replica"), 1),
    )
    summed = (
        lax.all_gather(spread[0], "replica", axis=0, tiled=True).astype(jnp.float32),
        lax.all_gather(spread[1], "replica", axis=1, tiled=True).astype(jnp.float32),
        lax.all_gather(spread[2], "replica", axis=0, tiled=True).astype(jnp.float32),
        lax.all_gather(spread[3], "replica", axis=1, tiled=True).astype(jnp.float32),
    )
    tensor_index = lax.axis_index("tensor")
    shard_index = lax.axis_index("shard")
    shard_count = lax.axis_size("shard")
    tensor_count = lax.axis_size("tensor")
    upbias_width = upbias_all.shape[0]
    qv_wide = lax.dynamic_update_slice(
        jnp.zeros((2, width), jnp.float32), g_qv, (0, tensor_index * cols)
    )
    upbias_wide = lax.dynamic_update_slice(
        jnp.zeros((upbias_width * tensor_count,), jnp.float32),
        g_upbias,
        (tensor_index * upbias_width,),
    )
    gain_tot, shift_tot, qv_tot, upbias_tot = lax.psum(
        (gain_part, shift_part, qv_wide, upbias_wide), ("tensor", "shard", "replica")
    )
    vec_piece = norm_gains.shape[1]
    qv_piece = qv_bias.shape[1]
    upbias_piece = up_bias.shape[0]
    owner_index = tensor_index * shard_count + shard_index
    grad_gains = lax.dynamic_slice_in_dim(gain_tot, shard_index * vec_piece, vec_piece, 1)
    grad_shifts = lax.dynamic_slice_in_dim(shift_tot, shard_index * vec_piece, vec_piece, 1)
    grad_qv = lax.dynamic_slice_in_dim(qv_tot, owner_index * qv_piece, qv_piece, 1)
    grad_upbias = lax.dynamic_slice_in_dim(upbias_tot, owner_index * upbias_piece, upbias_piece, 0)
    return (
        block_out,
        grad_in,
        summed[0],
        grad_qv,
        summed[1],
        summed[2],
        grad_upbias,
        summed[3],
        grad_gains,
        grad_shifts,
    )


def solution(mesh):
    in_specs = (
        P(("shard", "replica"), "tensor", None),
        P(("shard", "replica"), None),
        P(("shard", "replica"), "tensor", None),
        P("shard", None, "tensor"),
        P(None, ("tensor", "shard")),
        P("tensor", "shard"),
        P("shard", "tensor"),
        P(("tensor", "shard")),
        P("tensor", "shard"),
        P(None, "shard"),
        P(None, "shard"),
    )
    out_specs = (
        P(("shard", "replica"), "tensor", None),
        P(("shard", "replica"), "tensor", None),
        P("shard", None, "tensor"),
        P(None, ("tensor", "shard")),
        P("tensor", "shard"),
        P("shard", "tensor"),
        P(("tensor", "shard")),
        P("tensor", "shard"),
        P(None, "shard"),
        P(None, "shard"),
    )
    return jax.shard_map(shards, mesh=mesh, in_specs=in_specs, out_specs=out_specs, check_vma=False)
```

profile of v0, /device:TPU:0, one launch (start us, length us, event | category | flops | bytes accessed | tf_op | source)
XLA Modules:
  0.0 611.5 jit_solution(1188588645892185024)
XLA Ops:
  10.7 5.4 all-gather.1
  16.3 12.0 %all_gather.46 = bf16[256,1024]{1,0:T(8,128)(2,1)S(1)} all-gather(bf16[256,512]{1,0:T(8,128)(2,1)S(1)} %copy-done.16), channel_id=1, replica_groups=mesh['tensor'=4,'shard'=2,'replica'=4] {'shard'}, dimensions={1}, use_global_device_ids=true | all-gather | bytes 786432 | tf_op jit(solution)/shard_map/all_gather | solution.py:74
  28.6 12.7 %all-gather.14.cloned.1.call-done = bf16[1024,3,256]{0,2,1:T(8,128)(2,1)} async-done(((bf16[512,3,256]{0,2,1:T(8,128)(2,1)}), bf16[1024,3,256]{0,2,1:T(8,128)(2,1)}) %all-gather.14.cloned.1.call-update) | async-done | bytes 1572880 | tf_op jit(solution)/shard_map/all_gather | solution.py:72
  41.3 36.2 %all-gather.12.cloned.1.call-done = bf16[1,640,1024]{2,1,0:T(8,128)(2,1)} async-done(((bf16[1,160,1024]{2,1,0:T(8,128)(2,1)}), bf16[1,640,1024]{2,1,0:T(8,128)(2,1)}) %all-gather.12.cloned.1.call-update) | async-done | bytes 1310736 | tf_op jit(solution)/shard_map/all_gather | solution.py:91
  77.4 3.2 convolution_bitcast_fusion
  89.4 29.9 %reduce-scatter.15.cloned.1.call-done = bf16[1,160,1024]{2,1,0:T(8,128)(2,1)} async-done(((bf16[1,640,1024]{2,1,0:T(8,128)(2,1)}), bf16[1,160,1024]{2,1,0:T(8,128)(2,1)}) %reduce-scatter.15.cloned.1.call-update) | async-done | bytes 327696 | tf_op jit(solution)/shard_map/reduce_scatter | solution.py:35
  122.2 30.2 %all-gather.18.cloned.1.call-done = bf16[1024,1024]{1,0:T(8,128)(2,1)} async-done(((bf16[512,1024]{1,0:T(8,128)(2,1)}), bf16[1024,1024]{1,0:T(8,128)(2,1)}) %all-gather.18.cloned.1.call-update) | async-done | bytes 2097168 | tf_op jit(solution)/shard_map/all_gather | solution.py:75
  152.4 34.5 %all-gather.16.cloned.1.call-done = bf16[1,640,1024]{2,1,0:T(8,128)(2,1)} async-done(((bf16[1,160,1024]{2,1,0:T(8,128)(2,1)}), bf16[1,640,1024]{2,1,0:T(8,128)(2,1)}) %all-gather.16.cloned.1.call-update) | async-done | bytes 1310736 | tf_op jit(solution)/shard_map/all_gather | solution.py:125
  187.0 5.2 multiply_convert_fusion.1
  192.2 28.4 %all-gather.20.cloned.1.call-done = bf16[1024,1024]{1,0:T(8,128)(2,1)} async-done(((bf16[1024,512]{1,0:T(8,128)(2,1)}), bf16[1024,1024]{1,0:T(8,128)(2,1)}) %all-gather.20.cloned.1.call-update) | async-done | bytes 2097168 | tf_op jit(solution)/shard_map/all_gather | solution.py:77
  220.6 4.2 fusion.12
  224.9 31.5 %reduce-scatter.17.cloned.1.call-done = bf16[1,160,1024]{2,1,0:T(8,128)(2,1)} async-done(((bf16[1,640,1024]{2,1,0:T(8,128)(2,1)}), bf16[1,160,1024]{2,1,0:T(8,128)(2,1)}) %reduce-scatter.17.cloned.1.call-update) | async-done | bytes 327696 | tf_op jit(solution)/shard_map/reduce_scatter | solution.py:35
  260.2 31.1 %all-gather.22.cloned.1.call-done = bf16[1,640,1024]{2,1,0:T(8,128)(2,1)} async-done(((bf16[1,160,1024]{2,1,0:T(8,128)(2,1)}), bf16[1,640,1024]{2,1,0:T(8,128)(2,1)}) %all-gather.22.cloned.1.call-update) | async-done | bytes 1310736 | tf_op jit(solution)/shard_map/all_gather | solution.py:139
  291.4 5.9 fusion.55
  301.0 4.9 convolution_convert_fusion.1
  305.9 3.6 convolution_convert_fusion
  312.2 19.4 %reduce-scatter.19.cloned.1.call-done = bf16[1,160,1024]{2,1,0:T(8,128)(2,1)} async-done(((bf16[1,640,1024]{2,1,0:T(8,128)(2,1)}), bf16[1,160,1024]{2,1,0:T(8,128)(2,1)}) %reduce-scatter.19.cloned.1.call-update) | async-done | bytes 327696 | tf_op jit(solution)/shard_map/reduce_scatter | solution.py:35
  337.4 37.6 %reduce-scatter.23.cloned.1.call-done = bf16[128,1024]{1,0:T(8,128)(2,1)} async-done(((bf16[1024,1024]{1,0:T(8,128)(2,1)}), bf16[128,1024]{1,0:T(8,128)(2,1)}) %reduce-scatter.23.cloned.1.call-update) | async-done | bytes 262160 | tf_op jit(solution)/shard_map/reduce_scatter | solution.py:35
  375.2 44.9 %reduce-scatter.29.cloned.1.call-done = bf16[128,1024]{1,0:T(8,128)(2,1)} async-done(((bf16[1024,1024]{1,0:T(8,128)(2,1)}), bf16[128,1024]{1,0:T(8,128)(2,1)}) %reduce-scatter.29.cloned.1.call-update) | async-done | bytes 262160
  422.0 32.7 %all-gather.24.cloned.1.call-done = bf16[1,640,1024]{2,1,0:T(8,128)(2,1)} async-done(((bf16[1,160,1024]{2,1,0:T(8,128)(2,1)}), bf16[1,640,1024]{2,1,0:T(8,128)(2,1)}) %all-gather.24.cloned.1.call-update) | async-done | bytes 1310736 | tf_op jit(solution)/shard_map/all_gather | solution.py:175
  459.8 5.0 fusion.51
  464.8 4.0 multiply_reduce_fusion
  469.2 6.0 multiply_convert_fusion
  480.4 3.1 fusion.33
  484.6 3.0 convolution_convert_fusion.2
  489.3 3.7 fusion.11
  493.6 40.0 %all-reduce = (f32[2,1024]{1,0:T(2,128)S(1)}, f32[4096]{0:T(1024)S(1)}, f32[2,1024]{1,0:T(2,128)S(1)}, f32[4,1024]{1,0:T(4,128)S(1)}) all-reduce(f32[2,1024]{1,0:T(2,128)S(1)} %maximum_dynamic-update-slice_fusion, f32[4096]{0:T(1024)S(1)} %dynamic_update_slice.7, ...), channel_id=1, replica_groups=mesh['tensor'=4,'shard'=2,'replica'=4] {'tensor','shard','replica'}, use_global_device_ids=true, to_apply=%region_18.19 | all-reduce | flops 12288 | bytes 98304 | tf_op jit(solution)/shard_map/psum | solution.py:252
  538.8 2.9 convert_element_type.225
  542.7 6.5 %all_gather.53 = bf16[256,512]{1,0:T(8,128)(2,1)S(1)} all-gather(bf16[256,128]{1,0:T(8,128)(2,1)S(1)} %copy.63), channel_id=1, replica_groups=mesh['tensor'=4,'shard'=2,'replica'=4] {'replica'}, dimensions={1}, use_global_device_ids=true | all-gather | bytes 327680 | tf_op jit(solution)/shard_map/all_gather | solution.py:235
  550.0 19.5 %reduce-scatter.25.cloned.1.call-done = bf16[128,768]{1,0:T(8,128)(2,1)} async-done(((bf16[1024,768]{1,0:T(8,128)(2,1)}), bf16[128,768]{1,0:T(8,128)(2,1)}) %reduce-scatter.25.cloned.1.call-update) | async-done | bytes 196624
  570.6 8.6 %all_gather.52 = bf16[512,3,256]{0,2,1:T(8,128)(2,1)S(1)} all-gather(bf16[128,3,256]{0,2,1:T(8,128)(2,1)S(1)} %bitcast.140), channel_id=1, replica_groups=mesh['tensor'=4,'shard'=2,'replica'=4] {'replica'}, dimensions={0}, use_global_device_ids=true | all-gather | bytes 983040 | tf_op jit(solution)/shard_map/all_gather | solution.py:234
  580.6 22.5 %reduce-scatter.21.cloned.1.call-done = bf16[1,160,1024]{2,1,0:T(8,128)(2,1)} async-done(((bf16[1,640,1024]{2,1,0:T(8,128)(2,1)}), bf16[1,160,1024]{2,1,0:T(8,128)(2,1)}) %reduce-scatter.21.cloned.1.call-update) | async-done | bytes 327696 | tf_op jit(solution)/shard_map/reduce_scatter | solution.py:35
  (193 shorter events, 58.7 us)
Async XLA Ops:
  7.2 9.1 %copy-start.31 = (s32[1,640]{1,0:T(1,128)S(1)}, s32[1,640]{1,0:T(1,128)}, u32[]{:S(2)}) copy-start(s32[1,640]{1,0:T(1,128)} %param.12) | copy-start | bytes 7684
  7.2 9.1 %copy-start.16 = (bf16[256,512]{1,0:T(8,128)(2,1)S(1)}, bf16[256,512]{1,0:T(8,128)(2,1)}, u32[]{:S(2)}) copy-start(bf16[256,512]{1,0:T(8,128)(2,1)} %param.16) | copy-start | bytes 786436
  7.2 34.0 %all-gather.14.cloned.1.call-start = ((), (), s32[]{:S(2)}) async-start(), calls=%async_computation.9 | async-start | bytes 2359296 | tf_op jit(solution)/shard_map/all_gather | solution.py:72
  9.7 67.8 %all-gather.12.cloned.1.call-start = ((), (), s32[]{:S(2)}) async-start(), calls=%async_computation.8 | async-start | bytes 1638400 | tf_op jit(solution)/shard_map/all_gather | solution.py:91
  10.5 108.7 %reduce-scatter.15.cloned.1.call-start = ((), (), s32[]{:S(2)}) async-start(), calls=%async_computation.10 | async-start | bytes 1638400 | tf_op jit(solution)/shard_map/reduce_scatter | solution.py:35
  16.2 66.9 %copy-start.27 = (f32[4,64]{1,0:T(4,128)}, f32[4,64]{1,0:T(4,128)S(1)}, u32[]{:S(2)}) copy-start(f32[4,64]{1,0:T(4,128)S(1)} %add.169) | copy-start | bytes 3076
  28.3 58.0 %copy-start.11 = (bf16[256,1024]{1,0:T(8,128)(2,1)}, bf16[256,1024]{1,0:T(8,128)(2,1)S(1)}, u32[]{:S(2)}) copy-start(bf16[256,1024]{1,0:T(8,128)(2,1)S(1)} %all_gather.46) | copy-start | bytes 1572868
  88.6 63.8 %all-gather.18.cloned.1.call-start = ((), (), s32[]{:S(2)}) async-start(), calls=%async_computation.12 | async-start | bytes 3145728 | tf_op jit(solution)/shard_map/all_gather | solution.py:75
  89.2 97.8 %all-gather.16.cloned.1.call-start = ((), (), s32[]{:S(2)}) async-start(), calls=%async_computation.11 | async-start | bytes 1638400 | tf_op jit(solution)/shard_map/all_gather | solution.py:125
  121.6 99.1 %all-gather.20.cloned.1.call-start = ((), (), s32[]{:S(2)}) async-start(), calls=%async_computation.13 | async-start | bytes 3145728 | tf_op jit(solution)/shard_map/all_gather | solution.py:77
  122.1 134.2 %reduce-scatter.17.cloned.1.call-start = ((), (), s32[]{:S(2)}) async-start(), calls=%async_computation.14 | async-start | bytes 1638400 | tf_op jit(solution)/shard_map/reduce_scatter | solution.py:35
  192.2 28.4 %copy-start.36 = (bf16[640,1024]{1,0:T(8,128)(2,1)}, bf16[640,1024]{1,0:T(8,128)(2,1)S(1)}, u32[]{:S(2)}) copy-start(bf16[640,1024]{1,0:T(8,128)(2,1)S(1)} %get-tuple-element.78) | copy-start | bytes 3932164
  224.8 33.1 %copy-start.10 = (f32[1,160,1024]{2,1,0:T(8,128)S(1)}, f32[1,160,1024]{2,1,0:T(8,128)}, u32[]{:S(2)}) copy-start(f32[1,160,1024]{2,1,0:T(8,128)} %param.13) | copy-start | bytes 1966084
  224.8 66.5 %all-gather.22.cloned.1.call-start = ((), (), s32[]{:S(2)}) async-start(), calls=%async_computation.15 | async-start | bytes 1638400 | tf_op jit(solution)/shard_map/all_gather | solution.py:139
  260.0 71.6 %copy-start.4 = (f32[1,160,1024]{2,1,0:T(8,128)}, f32[1,160,1024]{2,1,0:T(8,128)S(1)}, u32[]{:S(2)}) copy-start(f32[1,160,1024]{2,1,0:T(8,128)S(1)} %get-tuple-element.58) | copy-start | bytes 1966084
  260.0 71.6 %reduce-scatter.19.cloned.1.call-start = ((), (), s32[]{:S(2)}) async-start(), calls=%async_computation.16 | async-start | bytes 1638400 | tf_op jit(solution)/shard_map/reduce_scatter | solution.py:35
  291.4 6.9 %copy-start.35 = (bf16[1024,1024]{1,0:T(8,128)(2,1)S(1)}, bf16[1024,1024]{1,0:T(8,128)(2,1)}, u32[]{:S(2)}) copy-start(bf16[1024,1024]{1,0:T(8,128)(2,1)} %all-gather.18.cloned.1.call-done) | copy-start | bytes 6291460
  300.9 74.1 %reduce-scatter.23.cloned.1.call-start = ((), (), s32[]{:S(2)}) async-start(), calls=%async_computation.19 | async-start | bytes 2359296 | tf_op jit(solution)/shard_map/reduce_scatter | solution.py:35
  305.9 114.2 %reduce-scatter.29.cloned.1.call-start = ((), (), s32[]{:S(2)}) async-start(), calls=%async_computation.24 | async-start | bytes 2359296
  312.1 142.5 %all-gather.24.cloned.1.call-start = ((), (), s32[]{:S(2)}) async-start(), calls=%async_computation.17 | async-start | bytes 1638400 | tf_op jit(solution)/shard_map/all_gather | solution.py:175
  333.6 131.2 %slice-start = ((s8[6553600]{0:T(1024)(128)(4,1)}), s8[2359296]{0:T(1024)(128)(4,1)S(1)}, s32[]{:S(2)}) async-start(s8[6553600]{0:T(1024)(128)(4,1)} %bitcast.122), calls=%async_computation.25 | async-start | bytes 4718592
  335.8 86.2 %copy-start.18 = (f32[4,640]{1,0:T(4,128)S(1)}, f32[4,640]{1,0:T(4,128)}, u32[]{:S(2)}) copy-start(f32[4,640]{1,0:T(4,128)} %copy-done.17) | copy-start | bytes 30724
  335.8 86.2 %copy-start.20 = (f32[4,640]{1,0:T(4,128)S(1)}, f32[4,640]{1,0:T(4,128)}, u32[]{:S(2)}) copy-start(f32[4,640]{1,0:T(4,128)} %copy-done.19) | copy-start | bytes 30724
  337.4 198.6 %all-gather.26.cloned.1.call-start = ((), (), s32[]{:S(2)}) async-start(), calls=%async_computation.20 | async-start | bytes 1310720 | tf_op jit(solution)/shard_map/all_gather | solution.py:236
  375.1 82.6 %copy-start.12 = (bf16[256,1024]{1,0:T(8,128)(2,1)S(1)}, bf16[256,1024]{1,0:T(8,128)(2,1)}, u32[]{:S(2)}) copy-start(bf16[256,1024]{1,0:T(8,128)(2,1)} %copy-done.11) | copy-start | bytes 1572868
  375.1 163.7 %all-gather.28.cloned.1.call-start = ((), (), s32[]{:S(2)}) async-start(), calls=%async_computation.21 | async-start | bytes 1310720 | tf_op jit(solution)/shard_map/all_gather | solution.py:237
  421.9 119.8 %reduce-scatter.27.cloned.1.call-start = ((), (), s32[]{:S(2)}) async-start(), calls=%async_computation.23 | async-start | bytes 589824
  457.7 7.1 %slice-start.1 = ((s8[6553600]{0:T(1024)(128)(4,1)}), s8[4194304]{0:T(1024)(128)(4,1)S(1)}, s32[]{:S(2)}) async-start(s8[6553600]{0:T(1024)(128)(4,1)} %bitcast.122), calls=%async_computation.26 | async-start | bytes 8388608
  468.9 100.6 %reduce-scatter.25.cloned.1.call-start = ((), (), s32[]{:S(2)}) async-start(), calls=%async_computation.22 | async-start | bytes 1769472
  469.2 6.0 copy-start.6
  489.2 113.8 %reduce-scatter.21.cloned.1.call-start = ((), (), s32[]{:S(2)}) async-start(), calls=%async_computation.18 | async-start | bytes 1638400 | tf_op jit(solution)/shard_map/reduce_scatter | solution.py:35
  549.1 53.9 %copy-start.3 = (f32[1,160,1024]{2,1,0:T(8,128)S(1)}, f32[1,160,1024]{2,1,0:T(8,128)}, u32[]{:S(2)}) copy-start(f32[1,160,1024]{2,1,0:T(8,128)} %copy-done.2) | copy-start | bytes 1966084
  (25 other events, 74.9 us)
Sparse Core Ops, SparseCore 0:
  10.2 31.0 all-gather.13
  43.4 33.9 all-gather.11
  88.7 30.4 reduce-scatter.14
  120.6 31.7 all-gather.17
  154.4 32.5 all-gather.15
  188.4 32.1 all-gather.19
  224.9 31.3 reduce-scatter.16
  260.1 31.1 all-gather.21
  301.1 30.4 reduce-scatter.18
  335.3 39.7 reduce-scatter.22
  378.9 41.1 reduce-scatter.28
  422.1 32.5 all-gather.23
  456.2 15.7 all-gather.25
  473.5 16.8 all-gather.27
  493.2 34.1 reduce-scatter.26
  531.1 38.3 reduce-scatter.24
  571.6 31.3 reduce-scatter.20
where the time goes:
time: 612 us; the launch traced here: 611 us
  waiting for transfers between devices  412 us (67%)
  blocking collectives  72.4 us (12%)
  matrix products  58.1 us (9%)
  other arithmetic  27.4 us (4%)
  local copies, waits for them, and re-layouts  25.5 us (4%)
  between operations  14.7 us (2%)
    reduce_scatter x5, waiting for transfers between devices, scatter_sum(): lax.psum_scatter(part.astype(jnp.bfloat16), axes, scatter_dimension=dim,...  141 us
    unnamed x20, waiting for transfers between devices  65.7 us
    psum x1, blocking collectives, shards(): lax.psum((gain_part, shift_part, qv_wide, upbias_wide), ('tensor', 'shard...  40 us
    all_gather x1, waiting for transfers between devices, shards(): input_rows_full = lax.all_gather(inputs_bf, 'tensor', axis=1, tiled=True)  36.2 us
    all_gather x1, waiting for transfers between devices, shards(): hidden_state_full = lax.all_gather(hidden_bf, 'tensor', axis=1, tiled=True)  34.5 us
    all_gather x1, waiting for transfers between devices, shards(): lax.all_gather(d_first.astype(jnp.bfloat16), 'tensor', axis=1, tiled=True)  32.7 us
    all_gather x1, waiting for transfers between devices, shards(): lax.all_gather(d_second.astype(jnp.bfloat16), 'tensor', axis=1, tiled=True)  31.1 us
    all_gather x1, waiting for transfers between devices, shards(): lax.all_gather(up_weight, 'shard', axis=0, tiled=True)  30.2 us
  transfers between devices with their start and end apart: 17, of which 14 were waited for; matrix products, arithmetic and copies ran while one was open for 13% of the time, Pallas kernels for 0%

commit v1 on v0

--- a/solution.py
+++ b/solution.py
@@ -250,7 +250,7 @@
         (tensor_index * upbias_width,),
     )
     gain_tot, shift_tot, qv_tot, upbias_tot = lax.psum(
-        (gain_part, shift_part, qv_wide, upbias_wide), ("tensor", "shard", "replica")
+        lax.psum((gain_part, shift_part, qv_wide, upbias_wide), ("shard", "replica")), "tensor"
     )
     vec_piece = norm_gains.shape[1]
     qv_piece = qv_bias.shape[1]

time: 612 us -> 612 us (level)
    psum x1 -> x2, blocking collectives: 40 us -> 42 us  [the longest x1 23.6 us: shards(): lax.psum((gain_part, shift_part, qv_wide, upbias_wide), ('shard', 'replic...]
where the time goes in v1:
time: 612 us; the launch traced here: 611 us
  waiting for transfers between devices  411 us (67%)
  blocking collectives  73.8 us (12%)
  matrix products  58.1 us (9%)
  other arithmetic  27.4 us (4%)
  local copies, waits for them, and re-layouts  25.4 us (4%)
  between operations  14.7 us (2%)
    reduce_scatter x5, waiting for transfers between devices, scatter_sum(): lax.psum_scatter(part.astype(jnp.bfloat16), axes, scatter_dimension=dim,...  141 us
    unnamed x20, waiting for transfers between devices  64.3 us
    all_gather x1, waiting for transfers between devices, shards(): input_rows_full = lax.all_gather(inputs_bf, 'tensor', axis=1, tiled=True)  36.2 us
    all_gather x1, waiting for transfers between devices, shards(): hidden_state_full = lax.all_gather(hidden_bf, 'tensor', axis=1, tiled=True)  34.5 us
    all_gather x1, waiting for transfers between devices, shards(): lax.all_gather(d_first.astype(jnp.bfloat16), 'tensor', axis=1, tiled=True)  32.6 us
    all_gather x1, waiting for transfers between devices, shards(): lax.all_gather(d_second.astype(jnp.bfloat16), 'tensor', axis=1, tiled=True)  31.1 us
    all_gather x1, waiting for transfers between devices, shards(): lax.all_gather(up_weight, 'shard', axis=0, tiled=True)  30.2 us
    all_gather x1, waiting for transfers between devices, shards(): lax.all_gather(down_weight, 'shard', axis=1, tiled=True)  28.4 us
  transfers between devices with their start and end apart: 17, of which 14 were waited for; matrix products, arithmetic and copies ran while one was open for 13% of the time, Pallas kernels for 0%

profile of v1, /device:TPU:0, one launch (start us, length us, event | category | flops | bytes accessed | tf_op | source)
XLA Modules:
  0.0 611.4 jit_solution(1714323254327031873)
XLA Ops:
  10.7 5.4 all-gather.1
  16.3 12.0 %all_gather.46 = bf16[256,1024]{1,0:T(8,128)(2,1)S(1)} all-gather(bf16[256,512]{1,0:T(8,128)(2,1)S(1)} %copy-done.16), channel_id=1, replica_groups=mesh['tensor'=4,'shard'=2,'replica'=4] {'shard'}, dimensions={1}, use_global_device_ids=true | all-gather | bytes 786432 | tf_op jit(solution)/shard_map/all_gather | solution.py:74
  28.6 12.7 %all-gather.14.cloned.1.call-done = bf16[1024,3,256]{0,2,1:T(8,128)(2,1)} async-done(((bf16[512,3,256]{0,2,1:T(8,128)(2,1)}), bf16[1024,3,256]{0,2,1:T(8,128)(2,1)}) %all-gather.14.cloned.1.call-update) | async-done | bytes 1572880 | tf_op jit(solution)/shard_map/all_gather | solution.py:72
  41.3 36.2 %all-gather.12.cloned.1.call-done = bf16[1,640,1024]{2,1,0:T(8,128)(2,1)} async-done(((bf16[1,160,1024]{2,1,0:T(8,128)(2,1)}), bf16[1,640,1024]{2,1,0:T(8,128)(2,1)}) %all-gather.12.cloned.1.call-update) | async-done | bytes 1310736 | tf_op jit(solution)/shard_map/all_gather | solution.py:91
  77.4 3.2 convolution_bitcast_fusion
  89.3 29.9 %reduce-scatter.15.cloned.1.call-done = bf16[1,160,1024]{2,1,0:T(8,128)(2,1)} async-done(((bf16[1,640,1024]{2,1,0:T(8,128)(2,1)}), bf16[1,160,1024]{2,1,0:T(8,128)(2,1)}) %reduce-scatter.15.cloned.1.call-update) | async-done | bytes 327696 | tf_op jit(solution)/shard_map/reduce_scatter | solution.py:35
  122.2 30.2 %all-gather.18.cloned.1.call-done = bf16[1024,1024]{1,0:T(8,128)(2,1)} async-done(((bf16[512,1024]{1,0:T(8,128)(2,1)}), bf16[1024,1024]{1,0:T(8,128)(2,1)}) %all-gather.18.cloned.1.call-update) | async-done | bytes 2097168 | tf_op jit(solution)/shard_map/all_gather | solution.py:75
  152.4 34.5 %all-gather.16.cloned.1.call-done = bf16[1,640,1024]{2,1,0:T(8,128)(2,1)} async-done(((bf16[1,160,1024]{2,1,0:T(8,128)(2,1)}), bf16[1,640,1024]{2,1,0:T(8,128)(2,1)}) %all-gather.16.cloned.1.call-update) | async-done | bytes 1310736 | tf_op jit(solution)/shard_map/all_gather | solution.py:125
  187.0 5.2 multiply_convert_fusion.1
  192.2 28.4 %all-gather.20.cloned.1.call-done = bf16[1024,1024]{1,0:T(8,128)(2,1)} async-done(((bf16[1024,512]{1,0:T(8,128)(2,1)}), bf16[1024,1024]{1,0:T(8,128)(2,1)}) %all-gather.20.cloned.1.call-update) | async-done | bytes 2097168 | tf_op jit(solution)/shard_map/all_gather | solution.py:77
  220.6 4.2 fusion.12
  224.8 31.5 %reduce-scatter.17.cloned.1.call-done = bf16[1,160,1024]{2,1,0:T(8,128)(2,1)} async-done(((bf16[1,640,1024]{2,1,0:T(8,128)(2,1)}), bf16[1,160,1024]{2,1,0:T(8,128)(2,1)}) %reduce-scatter.17.cloned.1.call-update) | async-done | bytes 327696 | tf_op jit(solution)/shard_map/reduce_scatter | solution.py:35
  260.2 31.1 %all-gather.22.cloned.1.call-done = bf16[1,640,1024]{2,1,0:T(8,128)(2,1)} async-done(((bf16[1,160,1024]{2,1,0:T(8,128)(2,1)}), bf16[1,640,1024]{2,1,0:T(8,128)(2,1)}) %all-gather.22.cloned.1.call-update) | async-done | bytes 1310736 | tf_op jit(solution)/shard_map/all_gather | solution.py:139
  291.3 5.9 fusion.55
  301.0 4.9 convolution_convert_fusion.1
  305.9 3.6 convolution_convert_fusion
  312.2 19.4 %reduce-scatter.19.cloned.1.call-done = bf16[1,160,1024]{2,1,0:T(8,128)(2,1)} async-done(((bf16[1,640,1024]{2,1,0:T(8,128)(2,1)}), bf16[1,160,1024]{2,1,0:T(8,128)(2,1)}) %reduce-scatter.19.cloned.1.call-update) | async-done | bytes 327696 | tf_op jit(solution)/shard_map/reduce_scatter | solution.py:35
  337.4 37.6 %reduce-scatter.23.cloned.1.call-done = bf16[128,1024]{1,0:T(8,128)(2,1)} async-done(((bf16[1024,1024]{1,0:T(8,128)(2,1)}), bf16[128,1024]{1,0:T(8,128)(2,1)}) %reduce-scatter.23.cloned.1.call-update) | async-done | bytes 262160 | tf_op jit(solution)/shard_map/reduce_scatter | solution.py:35
  375.1 45.0 %reduce-scatter.29.cloned.1.call-done = bf16[128,1024]{1,0:T(8,128)(2,1)} async-done(((bf16[1024,1024]{1,0:T(8,128)(2,1)}), bf16[128,1024]{1,0:T(8,128)(2,1)}) %reduce-scatter.29.cloned.1.call-update) | async-done | bytes 262160
  422.0 32.6 %all-gather.24.cloned.1.call-done = bf16[1,640,1024]{2,1,0:T(8,128)(2,1)} async-done(((bf16[1,160,1024]{2,1,0:T(8,128)(2,1)}), bf16[1,640,1024]{2,1,0:T(8,128)(2,1)}) %all-gather.24.cloned.1.call-update) | async-done | bytes 1310736 | tf_op jit(solution)/shard_map/all_gather | solution.py:175
  459.7 5.0 fusion.51
  464.8 4.0 multiply_reduce_fusion
  469.1 6.0 multiply_convert_fusion
  480.3 3.1 fusion.33
  484.5 3.0 convolution_convert_fusion.2
  489.3 3.7 fusion.11
  493.6 23.6 %all-reduce = (f32[2,1024]{1,0:T(2,128)S(1)}, f32[4096]{0:T(1024)S(1)}, f32[2,1024]{1,0:T(2,128)S(1)}, f32[4,1024]{1,0:T(4,128)S(1)}) all-reduce(f32[2,1024]{1,0:T(2,128)S(1)} %maximum_dynamic-update-slice_fusion, f32[4096]{0:T(1024)S(1)} %dynamic_update_slice.7, ...), channel_id=1, replica_groups=mesh['tensor'=4,'shard'=2,'replica'=4] {'shard','replica'}, use_global_device_ids=true, to_apply=%region_18.19 | all-reduce | flops 12288 | bytes 98304 | tf_op jit(solution)/shard_map/psum | solution.py:253
  517.1 18.4 %all-reduce.1 = (f32[2,1024]{1,0:T(2,128)S(1)}, f32[4096]{0:T(1024)S(1)}, f32[2,1024]{1,0:T(2,128)S(1)}, f32[4,1024]{1,0:T(4,128)S(1)}) all-reduce(f32[2,1024]{1,0:T(2,128)S(1)} %get-tuple-element.51, f32[4096]{0:T(1024)S(1)} %get-tuple-element.52, ...), channel_id=1, replica_groups=mesh['tensor'=4,'shard'=2,'replica'=4] {'tensor'}, use_global_device_ids=true, to_apply=%region_19.20 | all-reduce | flops 12288 | bytes 98304 | tf_op jit(solution)/shard_map/psum | solution.py:252
  544.7 5.8 all_gather.53
  551.3 18.1 %reduce-scatter.25.cloned.1.call-done = bf16[128,768]{1,0:T(8,128)(2,1)} async-done(((bf16[1024,768]{1,0:T(8,128)(2,1)}), bf16[128,768]{1,0:T(8,128)(2,1)}) %reduce-scatter.25.cloned.1.call-update) | async-done | bytes 196624
  570.5 8.6 %all_gather.52 = bf16[512,3,256]{0,2,1:T(8,128)(2,1)S(1)} all-gather(bf16[128,3,256]{0,2,1:T(8,128)(2,1)S(1)} %bitcast.140), channel_id=1, replica_groups=mesh['tensor'=4,'shard'=2,'replica'=4] {'replica'}, dimensions={0}, use_global_device_ids=true | all-gather | bytes 983040 | tf_op jit(solution)/shard_map/all_gather | solution.py:234
  580.5 22.5 %reduce-scatter.21.cloned.1.call-done = bf16[1,160,1024]{2,1,0:T(8,128)(2,1)} async-done(((bf16[1,640,1024]{2,1,0:T(8,128)(2,1)}), bf16[1,160,1024]{2,1,0:T(8,128)(2,1)}) %reduce-scatter.21.cloned.1.call-update) | async-done | bytes 327696 | tf_op jit(solution)/shard_map/reduce_scatter | solution.py:35
  (194 shorter events, 61.6 us)
Async XLA Ops:
  7.2 9.1 %copy-start.31 = (s32[1,640]{1,0:T(1,128)S(1)}, s32[1,640]{1,0:T(1,128)}, u32[]{:S(2)}) copy-start(s32[1,640]{1,0:T(1,128)} %param.12) | copy-start | bytes 7684
  7.2 9.1 %copy-start.16 = (bf16[256,512]{1,0:T(8,128)(2,1)S(1)}, bf16[256,512]{1,0:T(8,128)(2,1)}, u32[]{:S(2)}) copy-start(bf16[256,512]{1,0:T(8,128)(2,1)} %param.16) | copy-start | bytes 786436
  7.2 34.0 %all-gather.14.cloned.1.call-start = ((), (), s32[]{:S(2)}) async-start(), calls=%async_computation.9 | async-start | bytes 2359296 | tf_op jit(solution)/shard_map/all_gather | solution.py:72
  9.7 67.8 %all-gather.12.cloned.1.call-start = ((), (), s32[]{:S(2)}) async-start(), calls=%async_computation.8 | async-start | bytes 1638400 | tf_op jit(solution)/shard_map/all_gather | solution.py:91
  10.5 108.7 %reduce-scatter.15.cloned.1.call-start = ((), (), s32[]{:S(2)}) async-start(), calls=%async_computation.10 | async-start | bytes 1638400 | tf_op jit(solution)/shard_map/reduce_scatter | solution.py:35
  16.2 66.9 %copy-start.27 = (f32[4,64]{1,0:T(4,128)}, f32[4,64]{1,0:T(4,128)S(1)}, u32[]{:S(2)}) copy-start(f32[4,64]{1,0:T(4,128)S(1)} %add.177) | copy-start | bytes 3076
  28.3 58.0 %copy-start.11 = (bf16[256,1024]{1,0:T(8,128)(2,1)}, bf16[256,1024]{1,0:T(8,128)(2,1)S(1)}, u32[]{:S(2)}) copy-start(bf16[256,1024]{1,0:T(8,128)(2,1)S(1)} %all_gather.46) | copy-start | bytes 1572868
  88.6 63.8 %all-gather.18.cloned.1.call-start = ((), (), s32[]{:S(2)}) async-start(), calls=%async_computation.12 | async-start | bytes 3145728 | tf_op jit(solution)/shard_map/all_gather | solution.py:75
  89.2 97.8 %all-gather.16.cloned.1.call-start = ((), (), s32[]{:S(2)}) async-start(), calls=%async_computation.11 | async-start | bytes 1638400 | tf_op jit(solution)/shard_map/all_gather | solution.py:125
  121.5 99.1 %all-gather.20.cloned.1.call-start = ((), (), s32[]{:S(2)}) async-start(), calls=%async_computation.13 | async-start | bytes 3145728 | tf_op jit(solution)/shard_map/all_gather | solution.py:77
  122.1 134.2 %reduce-scatter.17.cloned.1.call-start = ((), (), s32[]{:S(2)}) async-start(), calls=%async_computation.14 | async-start | bytes 1638400 | tf_op jit(solution)/shard_map/reduce_scatter | solution.py:35
  192.2 28.4 %copy-start.36 = (bf16[640,1024]{1,0:T(8,128)(2,1)}, bf16[640,1024]{1,0:T(8,128)(2,1)S(1)}, u32[]{:S(2)}) copy-start(bf16[640,1024]{1,0:T(8,128)(2,1)S(1)} %get-tuple-element.82) | copy-start | bytes 3932164
  224.8 33.1 %copy-start.10 = (f32[1,160,1024]{2,1,0:T(8,128)S(1)}, f32[1,160,1024]{2,1,0:T(8,128)}, u32[]{:S(2)}) copy-start(f32[1,160,1024]{2,1,0:T(8,128)} %param.13) | copy-start | bytes 1966084
  224.8 66.5 %all-gather.22.cloned.1.call-start = ((), (), s32[]{:S(2)}) async-start(), calls=%async_computation.15 | async-start | bytes 1638400 | tf_op jit(solution)/shard_map/all_gather | solution.py:139
  260.0 71.6 %copy-start.4 = (f32[1,160,1024]{2,1,0:T(8,128)}, f32[1,160,1024]{2,1,0:T(8,128)S(1)}, u32[]{:S(2)}) copy-start(f32[1,160,1024]{2,1,0:T(8,128)S(1)} %get-tuple-element.62) | copy-start | bytes 1966084
  260.0 71.6 %reduce-scatter.19.cloned.1.call-start = ((), (), s32[]{:S(2)}) async-start(), calls=%async_computation.16 | async-start | bytes 1638400 | tf_op jit(solution)/shard_map/reduce_scatter | solution.py:35
  291.3 6.9 %copy-start.35 = (bf16[1024,1024]{1,0:T(8,128)(2,1)S(1)}, bf16[1024,1024]{1,0:T(8,128)(2,1)}, u32[]{:S(2)}) copy-start(bf16[1024,1024]{1,0:T(8,128)(2,1)} %all-gather.18.cloned.1.call-done) | copy-start | bytes 6291460
  300.9 74.1 %reduce-scatter.23.cloned.1.call-start = ((), (), s32[]{:S(2)}) async-start(), calls=%async_computation.19 | async-start | bytes 2359296 | tf_op jit(solution)/shard_map/reduce_scatter | solution.py:35
  305.9 114.2 %reduce-scatter.29.cloned.1.call-start = ((), (), s32[]{:S(2)}) async-start(), calls=%async_computation.24 | async-start | bytes 2359296
  312.1 142.5 %all-gather.24.cloned.1.call-start = ((), (), s32[]{:S(2)}) async-start(), calls=%async_computation.17 | async-start | bytes 1638400 | tf_op jit(solution)/shard_map/all_gather | solution.py:175
  333.6 131.2 %slice-start = ((s8[6553600]{0:T(1024)(128)(4,1)}), s8[2359296]{0:T(1024)(128)(4,1)S(1)}, s32[]{:S(2)}) async-start(s8[6553600]{0:T(1024)(128)(4,1)} %bitcast.122), calls=%async_computation.25 | async-start | bytes 4718592
  335.8 86.2 %copy-start.18 = (f32[4,640]{1,0:T(4,128)S(1)}, f32[4,640]{1,0:T(4,128)}, u32[]{:S(2)}) copy-start(f32[4,640]{1,0:T(4,128)} %copy-done.17) | copy-start | bytes 30724
  335.8 86.2 %copy-start.20 = (f32[4,640]{1,0:T(4,128)S(1)}, f32[4,640]{1,0:T(4,128)}, u32[]{:S(2)}) copy-start(f32[4,640]{1,0:T(4,128)} %copy-done.19) | copy-start | bytes 30724
  337.4 200.6 %all-gather.26.cloned.1.call-start = ((), (), s32[]{:S(2)}) async-start(), calls=%async_computation.20 | async-start | bytes 1310720 | tf_op jit(solution)/shard_map/all_gather | solution.py:236
  375.1 82.6 %copy-start.12 = (bf16[256,1024]{1,0:T(8,128)(2,1)S(1)}, bf16[256,1024]{1,0:T(8,128)(2,1)}, u32[]{:S(2)}) copy-start(bf16[256,1024]{1,0:T(8,128)(2,1)} %copy-done.11) | copy-start | bytes 1572868
  375.1 165.7 %all-gather.28.cloned.1.call-start = ((), (), s32[]{:S(2)}) async-start(), calls=%async_computation.21 | async-start | bytes 1310720 | tf_op jit(solution)/shard_map/all_gather | solution.py:237
  421.9 121.8 %reduce-scatter.27.cloned.1.call-start = ((), (), s32[]{:S(2)}) async-start(), calls=%async_computation.23 | async-start | bytes 589824
  457.6 7.1 %slice-start.1 = ((s8[6553600]{0:T(1024)(128)(4,1)}), s8[4194304]{0:T(1024)(128)(4,1)S(1)}, s32[]{:S(2)}) async-start(s8[6553600]{0:T(1024)(128)(4,1)} %bitcast.122), calls=%async_computation.26 | async-start | bytes 8388608
  468.9 100.6 %reduce-scatter.25.cloned.1.call-start = ((), (), s32[]{:S(2)}) async-start(), calls=%async_computation.22 | async-start | bytes 1769472
  469.1 6.0 copy-start.6
  489.2 113.8 %reduce-scatter.21.cloned.1.call-start = ((), (), s32[]{:S(2)}) async-start(), calls=%async_computation.18 | async-start | bytes 1638400 | tf_op jit(solution)/shard_map/reduce_scatter | solution.py:35
  550.5 52.5 %copy-start.3 = (f32[1,160,1024]{2,1,0:T(8,128)S(1)}, f32[1,160,1024]{2,1,0:T(8,128)}, u32[]{:S(2)}) copy-start(f32[1,160,1024]{2,1,0:T(8,128)} %copy-done.2) | copy-start | bytes 1966084
  (25 other events, 75.0 us)
Sparse Core Ops, SparseCore 0:
  10.2 31.0 all-gather.13
  43.4 33.9 all-gather.11
  88.7 30.4 reduce-scatter.14
  120.6 31.7 all-gather.17
  154.4 32.5 all-gather.15
  188.4 32.1 all-gather.19
  224.9 31.3 reduce-scatter.16
  260.1 31.1 all-gather.21
  301.1 30.4 reduce-scatter.18
  335.3 39.7 reduce-scatter.22
  378.9 41.1 reduce-scatter.28
  422.1 32.4 all-gather.23
  456.2 15.7 all-gather.25
  473.4 16.8 all-gather.27
  493.2 34.1 reduce-scatter.26
  531.1 38.3 reduce-scatter.24
  571.6 31.3 reduce-scatter.20
